TPU v7x, 512 devices: a whole 4x4x16 slice. The times are simulated.
512 devices in a mesh: seq: 4 (over y_lo, core), blk: 128 (over z, y_hi, x).
Axes of the slice: x: 4, y: 4 (y_hi: 2, y_lo: 2; y = y_hi * 2 + y_lo), z: 16, core: 2. Of those that a mesh axis runs over, the one named last changes fastest.
Arguments:
- tokens: bfloat16 [65536, 1024], P(('seq', 'blk')), may hold values from -6 to 6
- cotangent: bfloat16 [65536, 1024], P(('seq', 'blk')), may hold values from -6 to 6
- routes: int32 [65536, 2], P(('seq', 'blk')), may hold values from 0 to 63, all different within a row; in each aligned block of 128 rows (0 to 127, 128 to 255, ...) at most 8 rows name the same one
- gate_codes: int32 [65536, 2], P(('seq', 'blk')), may hold values from 1 to 64
- dropout_key: int32 [2], replicated, may hold values from 0 to 1073741823
- w_gate: bfloat16 [128, 1024, 352], P('blk', 'seq'), may hold values from -0.1875 to 0.1875
- w_up: bfloat16 [128, 1024, 352], P('blk', 'seq'), may hold values from -0.1875 to 0.1875
- w_down: bfloat16 [128, 352, 1024], P('blk', None, 'seq'), may hold values from -0.21875 to 0.21875
Outputs:
- layer_out: bfloat16 [65536, 1024], P(('seq', 'blk'))
- tokens_grad: bfloat16 [65536, 1024], P(('seq', 'blk'))
- gate_grad: bfloat16 [128, 1024, 352], P('blk', 'seq')
- up_grad: bfloat16 [128, 1024, 352], P('blk', 'seq')
- down_grad: bfloat16 [128, 352, 1024], P('blk', None, 'seq')
Inputs may be any that keep to these rules, and one draw needn't show every extreme that they name: `routes`: each row names 2 different experts; in the 128 rows of one device no expert is named more than 8 times.
All inputs are finite; a program needn't handle non-finite values.
Results may differ from a plain program's by a relative error of at most 0.0095.
Values may be sent and summed in bfloat16 or wider, within the bound.
A program may use at most 64 MiB of HBM per device.

v0:
```python
import jax
import jax.numpy as jnp
from jax import lax
from jax.sharding import PartitionSpec as P

mixing_factor = 73244475
contract_last = (((1,), (1,)), ((), ()))
contract_first = (((0,), (0,)), ((), ()))


def scramble(values):
    values = values ^ values >> 16 & 65535
    values = values * mixing_factor
    values = values ^ values >> 16 & 65535
    values = values * mixing_factor
    return values ^ values >> 16 & 65535


def keep_scale(token_ids, columns, key_pair):
    base_hash = scramble(key_pair[0] ^ scramble(key_pair[1]))
    mixed_ids = scramble(token_ids ^ base_hash)
    hashed = scramble(mixed_ids[:, None] ^ columns[None, :] * 40503)
    return jnp.where(hashed & 1023 >= 128, jnp.float32(8.0 / 7.0), jnp.float32(0.0))


def expert_pass(inputs_flat, cot_flat, ids_flat, gate_mat, up_mat, down_mat, columns, key_pair):
    drop_scale = keep_scale(ids_flat, columns, key_pair)
    gate_pre = jnp.dot(inputs_flat, gate_mat, preferred_element_type=jnp.float32)
    up_pre = jnp.dot(inputs_flat, up_mat, preferred_element_type=jnp.float32)
    sigmoid_gate = jax.nn.sigmoid(gate_pre)
    silu_gate = gate_pre * sigmoid_gate
    hidden = (silu_gate * up_pre * drop_scale).astype(jnp.bfloat16)
    expert_out = jnp.dot(hidden, down_mat, preferred_element_type=jnp.float32)
    hidden_grad = (
        lax.dot_general(cot_flat, down_mat, contract_last, preferred_element_type=jnp.float32)
        * drop_scale
    )
    gate_pre_grad = (
        hidden_grad * up_pre * sigmoid_gate * (1.0 + gate_pre * (1.0 - sigmoid_gate))
    ).astype(jnp.bfloat16)
    up_pre_grad = (hidden_grad * silu_gate).astype(jnp.bfloat16)
    input_grad = lax.dot_general(
        gate_pre_grad, gate_mat, contract_last, preferred_element_type=jnp.float32
    ) + lax.dot_general(up_pre_grad, up_mat, contract_last, preferred_element_type=jnp.float32)
    partial_gate = lax.dot_general(
        inputs_flat, gate_pre_grad, contract_first, preferred_element_type=jnp.float32
    )
    partial_up = lax.dot_general(
        inputs_flat, up_pre_grad, contract_first, preferred_element_type=jnp.float32
    )
    partial_down = lax.dot_general(
        hidden, cot_flat, contract_first, preferred_element_type=jnp.float32
    )
    return (expert_out, input_grad, partial_gate, partial_up, partial_down)


def local(tokens, cotangent, routes, gate_codes, dropout_key, w_gate, w_up, w_down):
    block_count = lax.axis_size("blk")
    seq_index = lax.axis_index("seq")
    blk_index = lax.axis_index("blk")
    tok_rows, model_width = tokens.shape
    top_count = routes.shape[1]
    expert_count = block_count // 2
    capacity = 2 * tok_rows * top_count // expert_count
    half_width = w_gate.shape[2]
    parity = blk_index % 2
    expert_here = blk_index // 2
    first_token = (seq_index * block_count + blk_index) * tok_rows
    token_ids = first_token + jnp.arange(tok_rows, dtype=jnp.int32)
    pair_expert = routes.reshape(-1)
    one_hot = (pair_expert[:, None] == jnp.arange(expert_count, dtype=jnp.int32)[None, :]).astype(
        jnp.int32
    )
    position = jnp.sum(jnp.cumsum(one_hot, axis=0) * one_hot, axis=1) - 1
    slot_index = pair_expert * capacity + position
    pair_gate = gate_codes.reshape(-1).astype(jnp.float32) / 64.0
    pair_inputs = jnp.repeat(tokens, top_count, axis=0)
    pair_cot = (
        pair_gate[:, None] * jnp.repeat(cotangent, top_count, axis=0).astype(jnp.float32)
    ).astype(jnp.bfloat16)
    slot_total = expert_count * capacity
    send_inputs = jnp.zeros((slot_total, model_width), jnp.bfloat16).at[slot_index].set(pair_inputs)
    send_cot = jnp.zeros((slot_total, model_width), jnp.bfloat16).at[slot_index].set(pair_cot)
    send_ids = (
        jnp.full((slot_total,), -1, jnp.int32).at[slot_index].set(jnp.repeat(token_ids, top_count))
    )
    gathered = (
        lax.all_gather(w_gate, "seq", axis=1, tiled=True),
        lax.all_gather(w_up, "seq", axis=1, tiled=True),
        lax.all_gather(w_down, "seq", axis=2, tiled=True),
    )
    gate_mat = gathered[0][0]
    up_mat = gathered[1][0]
    down_mat = gathered[2][0]
    half_columns = (
        expert_here * (2 * half_width)
        + parity * half_width
        + jnp.arange(half_width, dtype=jnp.int32)
    )

    def doubled(values):
        tail = values.shape[1:]
        shaped = values.reshape((expert_count, 1, capacity) + tail)
        return jnp.broadcast_to(shaped, (expert_count, 2, capacity) + tail).reshape(
            (block_count, capacity) + tail
        )

    recv_inputs, recv_cot, recv_ids = (
        lax.all_to_all(doubled(send_inputs), "blk", split_axis=0, concat_axis=0, tiled=True),
        lax.all_to_all(doubled(send_cot), "blk", split_axis=0, concat_axis=0, tiled=True),
        lax.all_to_all(doubled(send_ids), "blk", split_axis=0, concat_axis=0, tiled=True),
    )
    slot_rows = block_count * capacity
    expert_out, input_grad, partial_gate, partial_up, partial_down = expert_pass(
        recv_inputs.reshape(slot_rows, model_width),
        recv_cot.reshape(slot_rows, model_width),
        recv_ids.reshape(slot_rows),
        gate_mat,
        up_mat,
        down_mat,
        half_columns,
        dropout_key,
    )
    out_blocks = expert_out.reshape(block_count, capacity, model_width)
    grad_blocks = input_grad.reshape(block_count, capacity, model_width)
    returned = (
        lax.all_to_all(out_blocks, "blk", split_axis=0, concat_axis=0, tiled=True),
        lax.all_to_all(grad_blocks, "blk", split_axis=0, concat_axis=0, tiled=True),
    )

    def folded(values):
        return (
            values.reshape(expert_count, 2, capacity, model_width)
            .sum(axis=1)
            .reshape(slot_total, model_width)
        )

    slot_out = folded(returned[0])
    slot_grad = folded(returned[1])
    summed = (
        lax.psum_scatter(
            partial_gate.astype(jnp.bfloat16), "seq", scatter_dimension=0, tiled=True
        ).astype(jnp.float32),
        lax.psum_scatter(
            partial_up.astype(jnp.bfloat16), "seq", scatter_dimension=0, tiled=True
        ).astype(jnp.float32),
        lax.psum_scatter(
            partial_down.astype(jnp.bfloat16), "seq", scatter_dimension=1, tiled=True
        ).astype(jnp.float32),
    )
    pair_out = slot_out[slot_index].reshape(tok_rows, top_count, model_width)
    layer_out = jnp.sum(pair_gate.reshape(tok_rows, top_count, 1) * pair_out, axis=1).astype(
        jnp.bfloat16
    )
    tokens_grad = jnp.sum(
        slot_grad[slot_index].reshape(tok_rows, top_count, model_width), axis=1
    ).astype(jnp.bfloat16)
    gate_grad = summed[0].astype(jnp.bfloat16)[None]
    up_grad = summed[1].astype(jnp.bfloat16)[None]
    down_grad = summed[2].astype(jnp.bfloat16)[None]
    return (layer_out, tokens_grad, gate_grad, up_grad, down_grad)


def solution(mesh):
    placed = (
        P(("seq", "blk"), None),
        P(("seq", "blk"), None),
        P(("seq", "blk"), None),
        P(("seq", "blk"), None),
        P(),
        P("blk", "seq", None),
        P("blk", "seq", None),
        P("blk", None, "seq"),
    )
    return jax.shard_map(
        local,
        mesh=mesh,
        in_specs=placed,
        out_specs=(
            P(("seq", "blk"), None),
            P(("seq", "blk"), None),
            P("blk", "seq", None),
            P("blk", "seq", None),
            P("blk", None, "seq"),
        ),
        check_vma=False,
    )
```

profile of v0, /device:TPU:1, one launch (start us, length us, event | category | flops | bytes accessed | tf_op | source)
XLA Modules:
  0.0 685.2 jit_solution(7967179362408381233)
XLA Ops:
  7.2 0.7 broadcast_multiply_fusion
  7.9 0.8 copy.25
  8.6 0.1 eq.31
  8.8 0.1 eq.27
  8.9 0.1 copy.24
  9.1 0.1 mul.120
  9.2 0.1 broadcast_in_dim.63
  9.3 0.2 reshape.197
  9.4 0.6 reduce-window.6
  10.1 0.2 slice_reduce_fusion
  10.3 0.1 fusion.46
  10.4 1.4 scatter_custom_fusion.1
  11.8 0.1 broadcast_in_dim.64
  11.9 0.7 broadcast_in_dim.65
  12.6 23.0 %all-to-all-start.1 = ((s32[128,1,8]{2,1,0:T(1,128)}), s32[128,1,8]{2,1,0:T(1,128)S(1)}, u32[]{:S(2)}, u32[]{:S(2)}) async-start(s32[128,1,8]{2,1,0:T(1,128)} %bitcast.8), calls=%async_computation.1 | async-start | bytes 131072 | tf_op jit(solution)/shard_map/all_to_all | solution.py:111
  35.5 1.2 broadcast_in_dim.59
  36.7 0.2 reshape.189
  37.0 1.9 scatter_custom_fusion
  38.9 11.6 %all-to-all-done.1 = s32[128,1,8]{2,1,0:T(1,128)S(1)} async-done(((s32[128,1,8]{2,1,0:T(1,128)}), s32[128,1,8]{2,1,0:T(1,128)S(1)}, u32[]{:S(2)}, u32[]{:S(2)}) %all-to-all-start.1) | async-done | bytes 4128 | tf_op jit(solution)/shard_map/all_to_all | solution.py:111
  50.5 1.6 broadcast_in_dim.61
  52.1 7.5 %all-to-all-start = ((bf16[128,8,1024]{2,1,0:T(8,128)(2,1)}), bf16[128,8,1024]{2,1,0:T(8,128)(2,1)}, u32[]{:S(2)}, u32[]{:S(2)}) async-start(bf16[128,8,1024]{2,1,0:T(8,128)(2,1)} %bitcast.4), calls=%async_computation | async-start | bytes 4194304 | tf_op jit(solution)/shard_map/all_to_all | solution.py:109
  59.6 0.1 copy.23
  59.7 0.1 div.25
  59.9 0.3 broadcast_in_dim.68
  60.1 0.7 convert_element_type.60
  60.9 2.0 scatter_custom_fusion.2
  62.9 92.6 %all-to-all-done = bf16[128,8,1024]{2,1,0:T(8,128)(2,1)} async-done(((bf16[128,8,1024]{2,1,0:T(8,128)(2,1)}), bf16[128,8,1024]{2,1,0:T(8,128)(2,1)}, u32[]{:S(2)}, u32[]{:S(2)}) %all-to-all-start) | async-done | bytes 2097184 | tf_op jit(solution)/shard_map/all_to_all | solution.py:109
  155.5 1.6 broadcast_in_dim.70
  157.1 11.8 %all-to-all-start.3 = ((bf16[128,8,1024]{2,1,0:T(8,128)(2,1)}), bf16[128,8,1024]{2,1,0:T(8,128)(2,1)}, u32[]{:S(2)}, u32[]{:S(2)}) async-start(bf16[128,8,1024]{2,1,0:T(8,128)(2,1)} %bitcast.17), calls=%async_computation.3 | async-start | bytes 4194304 | tf_op jit(solution)/shard_map/all_to_all | solution.py:110
  169.0 0.6 fusion.50
  171.6 10.6 %all_gather.9 = bf16[1,1024,352]{1,2,0:T(8,128)(2,1)S(1)} all-gather(bf16[1,256,352]{1,2,0:T(8,128)(2,1)S(1)} %copy-done.5), channel_id=1, replica_groups=mesh['seq'=4,'blk'=128] {'seq'}, dimensions={1}, use_global_device_ids=true | all-gather | bytes 901120 | tf_op jit(solution)/shard_map/all_gather | solution.py:88
  182.1 9.4 %all_gather.10 = bf16[1,1024,352]{1,2,0:T(8,128)(2,1)S(1)} all-gather(bf16[1,256,352]{1,2,0:T(8,128)(2,1)S(1)} %copy-done.6), channel_id=1, replica_groups=mesh['seq'=4,'blk'=128] {'seq'}, dimensions={1}, use_global_device_ids=true | all-gather | bytes 901120 | tf_op jit(solution)/shard_map/all_gather | solution.py:89
  191.6 9.5 %all_gather.11 = bf16[1,352,1024]{2,1,0:T(8,128)(2,1)S(1)} all-gather(bf16[1,352,256]{2,1,0:T(8,128)(2,1)S(1)} %copy-done.7), channel_id=1, replica_groups=mesh['seq'=4,'blk'=128] {'seq'}, dimensions={2}, use_global_device_ids=true | all-gather | bytes 901120 | tf_op jit(solution)/shard_map/all_gather | solution.py:90
  201.0 0.2 xor_reduce_fusion
  201.2 0.1 xor.86
  201.3 3.6 fusion.8
  205.0 3.6 fusion.10
  208.6 56.2 %all-to-all-done.3 = bf16[128,8,1024]{2,1,0:T(8,128)(2,1)} async-done(((bf16[128,8,1024]{2,1,0:T(8,128)(2,1)}), bf16[128,8,1024]{2,1,0:T(8,128)(2,1)}, u32[]{:S(2)}, u32[]{:S(2)}) %all-to-all-start.3) | async-done | bytes 2097184 | tf_op jit(solution)/shard_map/all_to_all | solution.py:110
  264.8 5.7 multiply_convert_fusion
  270.5 1.5 copy.28
  272.0 3.2 fusion.31
  275.2 12.0 %all-to-all-start.2 = ((f32[128,8,1024]{2,1,0:T(8,128)}), f32[128,8,1024]{2,1,0:T(8,128)}, u32[]{:S(2)}, u32[]{:S(2)}) async-start(f32[128,8,1024]{2,1,0:T(8,128)} %fusion.31), calls=%async_computation.2 | async-start | bytes 8388608 | tf_op jit(solution)/shard_map/all_to_all | solution.py:127
  287.3 1.3 fusion.37
  288.6 3.3 add_bitcast_fusion
  291.9 180.3 %all-to-all-done.2 = f32[128,8,1024]{2,1,0:T(8,128)} async-done(((f32[128,8,1024]{2,1,0:T(8,128)}), f32[128,8,1024]{2,1,0:T(8,128)}, u32[]{:S(2)}, u32[]{:S(2)}) %all-to-all-start.2) | async-done | bytes 4194336 | tf_op jit(solution)/shard_map/all_to_all | solution.py:127
  472.2 13.3 %all-to-all-start.4 = ((f32[128,8,1024]{2,1,0:T(8,128)}), f32[128,8,1024]{2,1,0:T(8,128)}, u32[]{:S(2)}, u32[]{:S(2)}) async-start(f32[128,8,1024]{2,1,0:T(8,128)} %add_bitcast_fusion), calls=%async_computation.4 | async-start | bytes 8388608 | tf_op jit(solution)/shard_map/all_to_all | solution.py:128
  485.5 0.0 reduce-scatter.8.cloned.1.call-start
  485.5 3.4 fusion.28
  488.9 0.0 reduce-scatter.8.cloned.1.call-update
  488.9 0.0 reduce-scatter.4.cloned.1.call-start
  489.0 3.4 fusion.25
  492.4 0.0 reduce-scatter.4.cloned.1.call-update
  492.4 0.0 reduce-scatter.6.cloned.1.call-start
  492.4 3.4 fusion.22
  495.8 0.0 reduce-scatter.6.cloned.1.call-update
  495.9 2.8 bitcast_reduce_fusion.1
  498.7 1.1 gather_fusion
  499.7 1.6 reshape.162
  501.3 168.7 %all-to-all-done.4 = f32[128,8,1024]{2,1,0:T(8,128)} async-done(((f32[128,8,1024]{2,1,0:T(8,128)}), f32[128,8,1024]{2,1,0:T(8,128)}, u32[]{:S(2)}, u32[]{:S(2)}) %all-to-all-start.4) | async-done | bytes 4194336 | tf_op jit(solution)/shard_map/all_to_all | solution.py:128
  670.0 2.8 bitcast_reduce_fusion
  672.8 1.1 gather_fusion.1
  673.9 0.6 reshape.168
  674.5 2.1 reduce_sum.49
  676.6 2.1 multiply_reduce_fusion
  (33 shorter events, 0.1 us)
Async XLA Ops:
  12.6 37.9 %all-to-all-start.1 = ((s32[128,1,8]{2,1,0:T(1,128)}), s32[128,1,8]{2,1,0:T(1,128)S(1)}, u32[]{:S(2)}, u32[]{:S(2)}) async-start(s32[128,1,8]{2,1,0:T(1,128)} %bitcast.8), calls=%async_computation.1 | async-start | bytes 131072 | tf_op jit(solution)/shard_map/all_to_all | solution.py:111
  52.1 7.5 %copy-start.9 = (s32[128,2]{0,1:T(2,128)S(1)}, s32[128,2]{0,1:T(2,128)}, u32[]{:S(2)}) copy-start(s32[128,2]{0,1:T(2,128)} %param.11) | copy-start | bytes 3076
  52.1 7.8 %copy-start.4 = (bf16[128,1024]{1,0:T(8,128)(2,1)S(1)}, bf16[128,1024]{1,0:T(8,128)(2,1)}, u32[]{:S(2)}) copy-start(bf16[128,1024]{1,0:T(8,128)(2,1)} %param.9) | copy-start | bytes 786436
  52.1 103.4 %all-to-all-start = ((bf16[128,8,1024]{2,1,0:T(8,128)(2,1)}), bf16[128,8,1024]{2,1,0:T(8,128)(2,1)}, u32[]{:S(2)}, u32[]{:S(2)}) async-start(bf16[128,8,1024]{2,1,0:T(8,128)(2,1)} %bitcast.4), calls=%async_computation | async-start | bytes 4194304 | tf_op jit(solution)/shard_map/all_to_all | solution.py:109
  157.1 11.9 %copy-start.8 = (s32[2]{0:T(128)S(1)}, s32[2]{0:T(128)}, u32[]{:S(2)}) copy-start(s32[2]{0:T(128)} %param.12) | copy-start | bytes 28
  157.1 14.4 %copy-start.5 = (bf16[1,256,352]{1,2,0:T(8,128)(2,1)S(1)}, bf16[1,256,352]{1,2,0:T(8,128)(2,1)}, u32[]{:S(2)}) copy-start(bf16[1,256,352]{1,2,0:T(8,128)(2,1)} %param.13) | copy-start | bytes 540676
  157.1 25.0 %copy-start.6 = (bf16[1,256,352]{1,2,0:T(8,128)(2,1)S(1)}, bf16[1,256,352]{1,2,0:T(8,128)(2,1)}, u32[]{:S(2)}) copy-start(bf16[1,256,352]{1,2,0:T(8,128)(2,1)} %param.14) | copy-start | bytes 540676
  157.1 107.7 %all-to-all-start.3 = ((bf16[128,8,1024]{2,1,0:T(8,128)(2,1)}), bf16[128,8,1024]{2,1,0:T(8,128)(2,1)}, u32[]{:S(2)}, u32[]{:S(2)}) async-start(bf16[128,8,1024]{2,1,0:T(8,128)(2,1)} %bitcast.17), calls=%async_computation.3 | async-start | bytes 4194304 | tf_op jit(solution)/shard_map/all_to_all | solution.py:110
  168.9 22.6 %copy-start.7 = (bf16[1,352,256]{2,1,0:T(8,128)(2,1)S(1)}, bf16[1,352,256]{2,1,0:T(8,128)(2,1)}, u32[]{:S(2)}) copy-start(bf16[1,352,256]{2,1,0:T(8,128)(2,1)} %param.15) | copy-start | bytes 540676
  275.2 12.0 %copy-start.1 = (bf16[1024,352]{0,1:T(8,128)(2,1)S(1)}, bf16[1024,352]{0,1:T(8,128)(2,1)}, u32[]{:S(2)}) copy-start(bf16[1024,352]{0,1:T(8,128)(2,1)} %get-tuple-element.6) | copy-start | bytes 2162692
  275.2 196.9 %all-to-all-start.2 = ((f32[128,8,1024]{2,1,0:T(8,128)}), f32[128,8,1024]{2,1,0:T(8,128)}, u32[]{:S(2)}, u32[]{:S(2)}) async-start(f32[128,8,1024]{2,1,0:T(8,128)} %fusion.31), calls=%async_computation.2 | async-start | bytes 8388608 | tf_op jit(solution)/shard_map/all_to_all | solution.py:127
  287.2 1.3 copy-start.3
  291.9 193.7 %copy-start.2 = (bf16[1024,352]{0,1:T(8,128)(2,1)S(1)}, bf16[1024,352]{0,1:T(8,128)(2,1)}, u32[]{:S(2)}) copy-start(bf16[1024,352]{0,1:T(8,128)(2,1)} %get-tuple-element.7) | copy-start | bytes 2162692
  472.2 197.9 %all-to-all-start.4 = ((f32[128,8,1024]{2,1,0:T(8,128)}), f32[128,8,1024]{2,1,0:T(8,128)}, u32[]{:S(2)}, u32[]{:S(2)}) async-start(f32[128,8,1024]{2,1,0:T(8,128)} %add_bitcast_fusion), calls=%async_computation.4 | async-start | bytes 8388608 | tf_op jit(solution)/shard_map/all_to_all | solution.py:128
  485.5 193.2 %reduce-scatter.8.cloned.1.call-start = ((), (), s32[]{:S(2)}) async-start(), calls=%async_computation.10 | async-start | bytes 901120 | tf_op jit(solution)/shard_map/reduce_scatter | solution.py:147
  488.9 189.7 %reduce-scatter.4.cloned.1.call-start = ((), (), s32[]{:S(2)}) async-start(), calls=%async_computation.8 | async-start | bytes 901120 | tf_op jit(solution)/shard_map/reduce_scatter | solution.py:141
  492.4 186.3 %reduce-scatter.6.cloned.1.call-start = ((), (), s32[]{:S(2)}) async-start(), calls=%async_computation.9 | async-start | bytes 901120 | tf_op jit(solution)/shard_map/reduce_scatter | solution.py:144
  673.9 2.7 copy-start
Sparse Core Ops, SparseCore 0:
  489.7 29.7 reduce-scatter.7
  522.9 29.8 reduce-scatter.3
  556.2 28.7 reduce-scatter.5
where the time goes:
time: 689 us; the launch traced here: 685 us
  waiting for transfers between devices  509 us (74%)
  starting transfers between devices  67.7 us (10%)
  matrix products  31 us (4%)
  blocking collectives  29.5 us (4%)
  local copies, waits for them, and re-layouts  18.2 us (3%)
  between operations  16.1 us (2%)
  other arithmetic  13.4 us (2%)
    all_to_all x1, waiting for transfers between devices, local(): lax.all_to_all(out_blocks, 'blk', split_axis=0, concat_axis=0, tiled=True)  180 us
    all_to_all x1, waiting for transfers between devices, local(): lax.all_to_all(grad_blocks, 'blk', split_axis=0, concat_axis=0, tiled=True)  169 us
    all_to_all x1, waiting for transfers between devices, local(): lax.all_to_all(doubled(send_inputs), 'blk', split_axis=0, concat_axis=0,...  92.6 us
    all_to_all x1, waiting for transfers between devices, local(): lax.all_to_all(doubled(send_cot), 'blk', split_axis=0, concat_axis=0, til...  56.2 us
    all_to_all x1, starting transfers between devices, local(): lax.all_to_all(doubled(send_ids), 'blk', split_axis=0, concat_axis=0, til...  23 us
  transfers between devices with their start and end apart: 8, of which 5 were waited for; matrix products, arithmetic and copies ran while one was open for 6% of the time, Pallas kernels for 0%

commit v1 on v0

v1 whole, which is shorter than its diff:
```python
import jax
import jax.numpy as jnp
from jax import lax
from jax.sharding import PartitionSpec as P

mixing_factor = 73244475
contract_last = (((1,), (1,)), ((), ()))
contract_first = (((0,), (0,)), ((), ()))


def scramble(values):
    values = values ^ values >> 16 & 65535
    values = values * mixing_factor
    values = values ^ values >> 16 & 65535
    values = values * mixing_factor
    return values ^ values >> 16 & 65535


def keep_scale(token_ids, columns, key_pair):
    base_hash = scramble(key_pair[0] ^ scramble(key_pair[1]))
    mixed_ids = scramble(token_ids ^ base_hash)
    hashed = scramble(mixed_ids[:, None] ^ columns[None, :] * 40503)
    return jnp.where(hashed & 1023 >= 128, jnp.float32(8.0 / 7.0), jnp.float32(0.0))


def mm(a, b, dims=(((1,), (0,)), ((), ()))):
    return lax.dot_general(a, b, dims, preferred_element_type=jnp.float32)


def local(tokens, cotangent, routes, gate_codes, dropout_key, w_gate, w_up, w_down):
    block_count = lax.axis_size("blk")
    seq_index = lax.axis_index("seq")
    blk_index = lax.axis_index("blk")
    tok_rows, model_width = tokens.shape
    top_count = routes.shape[1]
    expert_count = block_count // 2
    capacity = 2 * tok_rows * top_count // expert_count
    part = capacity // 2
    half = w_gate.shape[2]
    parity = blk_index % 2
    expert_here = blk_index // 2
    bf = jnp.bfloat16

    pair_expert = routes.reshape(-1)
    one_hot = (pair_expert[:, None] == jnp.arange(expert_count, dtype=jnp.int32)[None, :]).astype(bf)
    pairs = tok_rows * top_count
    lower = (jnp.arange(pairs)[:, None] > jnp.arange(pairs)[None, :]).astype(bf)
    before = mm(lower, one_hot)
    position = jnp.sum(before * one_hot.astype(jnp.float32), axis=1).astype(jnp.int32)
    slot_index = (pair_expert * capacity + position).reshape(tok_rows, top_count)
    slot_total = expert_count * capacity
    slots = jnp.arange(slot_total, dtype=jnp.int32)
    gates = gate_codes.astype(jnp.float32) / 64.0
    hit = slots[:, None, None] == slot_index[None]
    select = jnp.sum(hit, axis=2).astype(bf)
    weigh = jnp.sum(jnp.where(hit, gates[None], 0.0), axis=2).astype(bf)
    local_ids = jnp.sum(jnp.where(hit, jnp.arange(tok_rows, dtype=jnp.int32)[None, :, None], 0), axis=(1, 2))

    send = jnp.concatenate([mm(select, tokens).astype(bf), mm(weigh, cotangent).astype(bf)], axis=1)
    send = send.reshape(block_count, part, 2 * model_width)
    recv_ids = lax.all_to_all(local_ids.reshape(block_count, part), "blk", 0, 0, tiled=True)
    recv = lax.all_to_all(send, "blk", split_axis=0, concat_axis=0, tiled=True)

    swap = [(i, i ^ 1) for i in range(block_count)]
    first = parity == 0

    def both(own):
        other = lax.ppermute(own, "blk", swap)
        return jnp.where(first, own, other), jnp.where(first, other, own)

    g0, g1 = both(w_gate[0])
    u0, u1 = both(w_up[0])
    d0, d1 = both(w_down[0])
    gate_mat = lax.all_gather(jnp.concatenate([g0, g1], axis=1), "seq", axis=0, tiled=True)
    up_mat = lax.all_gather(jnp.concatenate([u0, u1], axis=1), "seq", axis=0, tiled=True)
    down_mat = lax.all_gather(jnp.concatenate([d0, d1], axis=0), "seq", axis=1, tiled=True)

    rows = block_count * part
    row_ids = (
        (seq_index * block_count + jnp.arange(block_count, dtype=jnp.int32)) * tok_rows
    )[:, None] + recv_ids
    row_ids = row_ids.reshape(rows)
    columns = expert_here * (2 * half) + jnp.arange(2 * half, dtype=jnp.int32)
    recv = recv.reshape(rows, 2 * model_width)
    inputs = recv[:, :model_width]
    cot = recv[:, model_width:]

    drop = keep_scale(row_ids, columns, dropout_key)
    gate_pre = mm(inputs, gate_mat)
    up_pre = mm(inputs, up_mat)
    sig = jax.nn.sigmoid(gate_pre)
    silu = gate_pre * sig
    hidden = (silu * up_pre * drop).astype(bf)
    expert_out = mm(hidden, down_mat).astype(bf)
    hidden_grad = mm(cot, down_mat, contract_last) * drop
    gate_pre_grad = (hidden_grad * up_pre * sig * (1.0 + gate_pre * (1.0 - sig))).astype(bf)
    up_pre_grad = (hidden_grad * silu).astype(bf)
    input_grad = (mm(gate_pre_grad, gate_mat, contract_last) + mm(up_pre_grad, up_mat, contract_last)).astype(bf)

    back = jnp.concatenate([expert_out, input_grad], axis=1).reshape(block_count, part, 2 * model_width)
    returned = lax.all_to_all(back, "blk", split_axis=0, concat_axis=0, tiled=True)

    part_gate = mm(inputs, gate_pre_grad, contract_first)
    part_up = mm(inputs, up_pre_grad, contract_first)
    part_down = mm(hidden, cot, contract_first)

    def paired(low, high):
        theirs = jnp.where(first, high, low).astype(bf)
        ours = jnp.where(first, low, high)
        return (ours + lax.ppermute(theirs, "blk", swap).astype(jnp.float32)).astype(bf)

    gate_grad = lax.psum_scatter(paired(part_gate[:, :half], part_gate[:, half:]), "seq", scatter_dimension=0, tiled=True)
    up_grad = lax.psum_scatter(paired(part_up[:, :half], part_up[:, half:]), "seq", scatter_dimension=0, tiled=True)
    down_grad = lax.psum_scatter(paired(part_down[:half], part_down[half:]), "seq", scatter_dimension=1, tiled=True)

    returned = returned.reshape(slot_total, 2 * model_width)
    layer_out = mm(weigh, returned[:, :model_width], contract_first).astype(bf)
    tokens_grad = mm(select, returned[:, model_width:], contract_first).astype(bf)
    return (layer_out, tokens_grad, gate_grad[None], up_grad[None], down_grad[None])


def solution(mesh):
    rows = P(("seq", "blk"), None)
    wide = P("blk", "seq", None)
    down = P("blk", None, "seq")
    return jax.shard_map(
        local,
        mesh=mesh,
        in_specs=(rows, rows, rows, rows, P(), wide, wide, down),
        out_specs=(rows, rows, wide, wide, down),
        check_vma=False,
    )
```

time: 689 us -> 342 us (0.50)
  waiting for transfers between devices: 509 us -> 211 us
  blocking collectives: 29.5 us -> 0 us
  matrix products: 31 us -> 22.7 us
    all_to_all x5 -> x3, waiting for transfers between devices: 509 us -> 96.5 us  [the longest x1 68.7 us: local(): recv = lax.all_to_all(send, 'blk', split_axis=0, concat_axis=0, tiled=True)]
    ppermute x0 -> x6, waiting for transfers between devices: none -> 77.8 us  [the longest x3 65.7 us: paired(): lax.ppermute(theirs, 'blk', swap).astype(jnp.float32)]
    all_gather x3 -> x0, blocking collectives: 29.5 us -> none  [the longest x1 10.6 us: local(): lax.all_gather(w_gate, 'seq', axis=1, tiled=True)]
    all_gather x0 -> x3, waiting for transfers between devices: none -> 18.9 us  [the longest x1 18.9 us: local(): lax.all_gather(jnp.concatenate([u0, u1], axis=1), 'seq', axis=0, tiled=True)]
    all_to_all x5 -> x3, starting transfers between devices: 67.5 us -> 50.1 us  [the longest x1 22.9 us: local(): lax.all_to_all(local_ids.reshape(block_count, part), 'blk', 0, 0, tiled=T...]
    reduce_scatter x3, waiting for transfers between devices: 0.01 us -> 17.3 us  [the longest x1 17.3 us: local(): lax.psum_scatter(paired(part_down[:half], part_down[half:]), 'seq', scatt...]
    ppermute x0 -> x6, starting transfers between devices: none -> 14 us  [the longest x3 7.71 us: both(): other = lax.ppermute(own, 'blk', swap)]
    reduce_sum x5 -> x2, other arithmetic: 9.84 us -> 0.23 us  [the longest x1 0.17 us: local(): jnp.sum(jnp.where(hit, jnp.arange(tok_rows, dtype=jnp.int32)[None, :, Non...]
  transfers between devices with their start and end apart: 8 -> 15, of which waited for: 5 -> 11; matrix products, arithmetic and copies ran while one was open for 6% -> 9% of each run, Pallas kernels for 0% -> 0%
where the time goes in v1:
time: 342 us; the launch traced here: 341 us
  waiting for transfers between devices  211 us (62%)
  starting transfers between devices  64.5 us (19%)
  matrix products  22.7 us (7%)
  between operations  16.5 us (5%)
  local copies, waits for them, and re-layouts  16 us (5%)
  other arithmetic  10.8 us (3%)
    all_to_all x1, waiting for transfers between devices, local(): recv = lax.all_to_all(send, 'blk', split_axis=0, concat_axis=0, tiled=True)  68.7 us
    ppermute x3, waiting for transfers between devices, paired(): lax.ppermute(theirs, 'blk', swap).astype(jnp.float32)  65.7 us
    all_to_all x1, starting transfers between devices, local(): lax.all_to_all(local_ids.reshape(block_count, part), 'blk', 0, 0, tiled=T...  22.9 us
    dot_general x14, matrix products, mm(): return lax.dot_general(a, b, dims, preferred_element_type=jnp.float32)  22.7 us
    all_to_all x1, starting transfers between devices, local(): lax.all_to_all(back, 'blk', split_axis=0, concat_axis=0, tiled=True)  19.3 us
    all_gather x1, waiting for transfers between devices, local(): lax.all_gather(jnp.concatenate([u0, u1], axis=1), 'seq', axis=0, tiled=True)  18.9 us
    reduce_scatter x1, waiting for transfers between devices, local(): lax.psum_scatter(paired(part_down[:half], part_down[half:]), 'seq', scatt...  17.3 us
    all_to_all x1, waiting for transfers between devices, local(): lax.all_to_all(back, 'blk', split_axis=0, concat_axis=0, tiled=True)  16.9 us
  transfers between devices with their start and end apart: 15, of which 11 were waited for; matrix products, arithmetic and copies ran while one was open for 9% of the time, Pallas kernels for 0%

profile of v1, /device:TPU:1, one launch (start us, length us, event | category | flops | bytes accessed | tf_op | source)
XLA Modules:
  0.0 341.1 jit_solution(9207838487095601653)
XLA Ops:
  7.2 0.8 copy.29
  8.0 0.1 eq.34
  8.2 0.2 fusion.8
  8.4 0.1 convert_element_type.84
  8.6 0.7 multiply_add_fusion
  9.3 0.2 select_reduce_fusion
  9.5 0.7 all_to_all.15
  10.2 22.9 %all-to-all-start.1 = ((s32[128,1,4]{2,1,0:T(1,128)}), s32[128,1,4]{2,1,0:T(1,128)S(1)}, u32[]{:S(2)}, u32[]{:S(2)}) async-start(s32[128,1,4]{2,1,0:T(1,128)} %bitcast.2), calls=%async_computation.1 | async-start | bytes 131072 | tf_op jit(solution)/shard_map/all_to_all | solution.py:61
  33.2 0.7 convert_multiply_fusion
  33.9 0.4 convolution_convert_fusion.1
  34.4 0.4 convolution_convert_fusion
  34.8 0.2 pad_maximum_fusion
  35.0 2.3 reshape.72
  37.3 10.8 %all-to-all-done.1 = s32[128,1,4]{2,1,0:T(1,128)S(1)} async-done(((s32[128,1,4]{2,1,0:T(1,128)}), s32[128,1,4]{2,1,0:T(1,128)S(1)}, u32[]{:S(2)}, u32[]{:S(2)}) %all-to-all-start.1) | async-done | bytes 2080 | tf_op jit(solution)/shard_map/all_to_all | solution.py:61
  48.1 7.8 %all-to-all-start = ((bf16[128,4,2048]{2,1,0:T(4,128)(2,1)}), bf16[128,4,2048]{2,1,0:T(4,128)(2,1)}, u32[]{:S(2)}, u32[]{:S(2)}) async-start(bf16[128,4,2048]{2,1,0:T(4,128)(2,1)} %reshape.72), calls=%async_computation | async-start | bytes 4194304 | tf_op jit(solution)/shard_map/all_to_all | solution.py:62
  56.0 2.5 collective-permute-start.1
  58.6 2.9 collective-permute-start
  61.5 1.5 collective-permute-done.1
  63.0 5.9 %collective-permute-done = bf16[256,352]{0,1:T(8,128)(2,1)S(1)} collective-permute-done((bf16[256,352]{0,1:T(8,128)(2,1)S(1)}, bf16[256,352]{0,1:T(8,128)(2,1)S(1)}, u32[]{:S(2)}, u32[]{:S(2)}) %collective-permute-start) | collective-permute-done | bytes 180256 | tf_op jit(solution)/shard_map/ppermute | solution.py:68
  68.9 0.8 pad_maximum_fusion.2
  69.8 2.3 collective-permute-start.2
  72.1 4.8 %collective-permute-done.2 = bf16[352,256]{1,0:T(8,128)(2,1)S(1)} collective-permute-done((bf16[352,256]{1,0:T(8,128)(2,1)S(1)}, bf16[352,256]{1,0:T(8,128)(2,1)S(1)}, u32[]{:S(2)}, u32[]{:S(2)}) %collective-permute-start.2) | collective-permute-done | bytes 180256 | tf_op jit(solution)/shard_map/ppermute | solution.py:68
  76.9 0.8 pad_maximum_fusion.4
  77.7 0.2 all-gather.6.cloned.1.call-start
  77.9 0.8 pad_maximum_fusion.3
  78.8 0.6 fusion.28
  81.4 0.1 add.75
  81.5 0.5 broadcast.116
  82.0 0.8 reduce.3
  82.9 0.1 all_to_all.17
  83.0 68.7 %all-to-all-done = bf16[128,4,2048]{2,1,0:T(4,128)(2,1)} async-done(((bf16[128,4,2048]{2,1,0:T(4,128)(2,1)}), bf16[128,4,2048]{2,1,0:T(4,128)(2,1)}, u32[]{:S(2)}, u32[]{:S(2)}) %all-to-all-start) | async-done | bytes 2097184 | tf_op jit(solution)/shard_map/all_to_all | solution.py:62
  151.7 2.5 reshape.73
  154.3 3.5 %fusion.20 = f32[512,704]{0,1:T(8,128)} fusion(bf16[1024,704]{0,1:T(8,128)(2,1)} %all-gather.4.cloned.1.call-done, bf16[512,2048]{1,0:T(8,128)(2,1)S(1)} %reshape.73), kind=kOutput, calls=%fused_computation.43 | convolution fusion | flops 738197504 | bytes 3932160 | tf_op jit(solution)/shard_map/dot_general | solution.py:27
  157.8 3.8 %select_multiply_fusion = f32[512,704]{0,1:T(8,128)} fusion(bf16[704,1024]{1,0:T(8,128)(2,1)} %all-gather.8.cloned.1.call-done, bf16[512,2048]{1,0:T(8,128)(2,1)S(1)} %reshape.73, s32[704]{0:T(1024)S(1)} %add_multiply_fusion, s32[512]{0:T(512)S(1)} %and_xor_fusion), kind=kOutput, calls=%fused_computation.5 | convolution fusion | flops 743964672 | bytes 3938304 | tf_op jit(solution)/shard_map/dot_general | solution.py:27
  161.5 18.9 %all-gather.6.cloned.1.call-done = bf16[1024,704]{0,1:T(8,128)(2,1)} async-done(((bf16[256,704]{0,1:T(8,128)(2,1)}), bf16[1024,704]{0,1:T(8,128)(2,1)}) %all-gather.6.cloned.1.call-update) | async-done | bytes 1441808 | tf_op jit(solution)/shard_map/all_gather | solution.py:75
  180.4 4.4 %fusion = (bf16[512,704]{0,1:T(8,128)(2,1)S(1)}, bf16[512,704]{0,1:T(8,128)(2,1)S(1)}, bf16[512,704]{0,1:T(8,128)(2,1)S(1)}) fusion(s32[704]{0:T(1024)S(1)} %add_multiply_fusion, s32[512]{0:T(512)S(1)} %and_xor_fusion, f32[512,704]{0,1:T(8,128)} %fusion.20, f32[512,704]{0,1:T(8,128)} %select_multiply_fusion, ...), kind=kOutput, calls=%fused_computation.10 | convolution fusion | flops 749371392 | bytes 7542784 | tf_op jit(solution)/shard_map/dot_general | solution.py:27
  184.8 1.0 convolution_convert_fusion.2
  185.8 0.8 copy-done.10
  186.7 1.0 fusion.29
  187.7 0.3 copy-done.8
  188.1 1.0 add_convert_fusion
  189.1 1.5 pad_maximum_fusion.1
  190.6 4.1 %reshape.74 = bf16[128,4,2048]{2,1,0:T(4,128)(2,1)} reshape(bf16[512,2048]{1,0:T(8,128)(2,1)} %pad_maximum_fusion.1) | data formatting | bytes 4194304 | tf_op jit(solution)/shard_map/reshape | solution.py:100
  194.7 19.3 %all-to-all-start.2 = ((bf16[128,4,2048]{2,1,0:T(4,128)(2,1)}), bf16[128,4,2048]{2,1,0:T(4,128)(2,1)}, u32[]{:S(2)}, u32[]{:S(2)}) async-start(bf16[128,4,2048]{2,1,0:T(4,128)(2,1)} %reshape.74), calls=%async_computation.2 | async-start | bytes 4194304 | tf_op jit(solution)/shard_map/all_to_all | solution.py:101
  214.1 2.0 fusion.14
  216.1 0.1 select_convert_fusion.2
  216.2 2.4 collective-permute-start.3
  218.6 21.6 %collective-permute-done.3 = bf16[1024,352]{0,1:T(8,128)(2,1)S(1)} collective-permute-done((bf16[1024,352]{0,1:T(8,128)(2,1)S(1)}, bf16[1024,352]{0,1:T(8,128)(2,1)S(1)}, u32[]{:S(2)}, u32[]{:S(2)}) %collective-permute-start.3) | collective-permute-done | bytes 720928 | tf_op jit(solution)/shard_map/ppermute | solution.py:110
  240.3 1.3 add_convert_fusion.3
  241.6 2.0 fusion.16
  243.6 0.1 select_convert_fusion.1
  243.8 1.9 collective-permute-start.4
  245.7 22.5 %collective-permute-done.4 = bf16[1024,352]{0,1:T(8,128)(2,1)S(1)} collective-permute-done((bf16[1024,352]{0,1:T(8,128)(2,1)S(1)}, bf16[1024,352]{0,1:T(8,128)(2,1)S(1)}, u32[]{:S(2)}, u32[]{:S(2)}) %collective-permute-start.4) | collective-permute-done | bytes 720928 | tf_op jit(solution)/shard_map/ppermute | solution.py:110
  268.2 1.3 add_convert_fusion.2
  269.5 0.9 fusion.11
  270.4 0.1 select_convert_fusion
  270.6 1.9 collective-permute-start.5
  272.5 21.6 %collective-permute-done.5 = bf16[352,1024]{1,0:T(8,128)(2,1)S(1)} collective-permute-done((bf16[352,1024]{1,0:T(8,128)(2,1)S(1)}, bf16[352,1024]{1,0:T(8,128)(2,1)S(1)}, u32[]{:S(2)}, u32[]{:S(2)}) %collective-permute-start.5) | collective-permute-done | bytes 720928 | tf_op jit(solution)/shard_map/ppermute | solution.py:110
  294.1 1.3 add_convert_fusion.1
  295.4 16.9 %all-to-all-done.2 = bf16[128,4,2048]{2,1,0:T(4,128)(2,1)} async-done(((bf16[128,4,2048]{2,1,0:T(4,128)(2,1)}), bf16[128,4,2048]{2,1,0:T(4,128)(2,1)}, u32[]{:S(2)}, u32[]{:S(2)}) %all-to-all-start.2) | async-done | bytes 2097184 | tf_op jit(solution)/shard_map/all_to_all | solution.py:101
  312.4 2.5 reshape.75
  314.9 1.0 convolution_convert_fusion.4
  315.9 1.0 convolution_convert_fusion.3
  317.0 17.3 %reduce-scatter.8.cloned.1.call-done = bf16[352,256]{1,0:T(8,128)(2,1)} async-done(((bf16[352,1024]{1,0:T(8,128)(2,1)}), bf16[352,256]{1,0:T(8,128)(2,1)}) %reduce-scatter.8.cloned.1.call-update) | async-done | bytes 180240 | tf_op jit(solution)/shard_map/reduce_scatter | solution.py:114
  (44 shorter events, 0.7 us)
Async XLA Ops:
  7.2 26.8 %copy-start = (bf16[128,1024]{1,0:T(8,128)(2,1)S(1)}, bf16[128,1024]{1,0:T(8,128)(2,1)}, u32[]{:S(2)}) copy-start(bf16[128,1024]{1,0:T(8,128)(2,1)} %param.8) | copy-start | bytes 786436
  7.2 27.2 %copy-start.3 = (bf16[128,1024]{1,0:T(8,128)(2,1)S(1)}, bf16[128,1024]{1,0:T(8,128)(2,1)}, u32[]{:S(2)}) copy-start(bf16[128,1024]{1,0:T(8,128)(2,1)} %param.9) | copy-start | bytes 786436
  10.2 37.9 %all-to-all-start.1 = ((s32[128,1,4]{2,1,0:T(1,128)}), s32[128,1,4]{2,1,0:T(1,128)S(1)}, u32[]{:S(2)}, u32[]{:S(2)}) async-start(s32[128,1,4]{2,1,0:T(1,128)} %bitcast.2), calls=%async_computation.1 | async-start | bytes 131072 | tf_op jit(solution)/shard_map/all_to_all | solution.py:61
  37.3 18.7 %copy-start.4 = (bf16[1,256,352]{1,2,0:T(8,128)(2,1)S(1)}, bf16[1,256,352]{1,2,0:T(8,128)(2,1)}, u32[]{:S(2)}) copy-start(bf16[1,256,352]{1,2,0:T(8,128)(2,1)} %param.14) | copy-start | bytes 540676
  37.3 21.3 %copy-start.5 = (bf16[1,256,352]{1,2,0:T(8,128)(2,1)S(1)}, bf16[1,256,352]{1,2,0:T(8,128)(2,1)}, u32[]{:S(2)}) copy-start(bf16[1,256,352]{1,2,0:T(8,128)(2,1)} %param.13) | copy-start | bytes 540676
  48.1 103.6 %all-to-all-start = ((bf16[128,4,2048]{2,1,0:T(4,128)(2,1)}), bf16[128,4,2048]{2,1,0:T(4,128)(2,1)}, u32[]{:S(2)}, u32[]{:S(2)}) async-start(bf16[128,4,2048]{2,1,0:T(4,128)(2,1)} %reshape.72), calls=%async_computation | async-start | bytes 4194304 | tf_op jit(solution)/shard_map/all_to_all | solution.py:62
  55.9 13.9 %copy-start.6 = (bf16[1,352,256]{2,1,0:T(8,128)(2,1)S(1)}, bf16[1,352,256]{2,1,0:T(8,128)(2,1)}, u32[]{:S(2)}) copy-start(bf16[1,352,256]{2,1,0:T(8,128)(2,1)} %param.15) | copy-start | bytes 540676
  55.9 98.3 %all-gather.4.cloned.1.call-start = ((), (), s32[]{:S(2)}) async-start(), calls=%async_computation.6 | async-start | bytes 1802240 | tf_op jit(solution)/shard_map/all_gather | solution.py:74
  56.0 7.0 %collective-permute-start.1 = (bf16[256,352]{0,1:T(8,128)(2,1)S(1)}, bf16[256,352]{0,1:T(8,128)(2,1)S(1)}, u32[]{:S(2)}, u32[]{:S(2)}) collective-permute-start(bf16[256,352]{0,1:T(8,128)(2,1)S(1)} %bitcast.31), channel_id=1, source_target_pairs={{0,1},{1,0},{2,3},{3,2},{4,5},{5,4},{6,7},{7,6},{8,9},{9,8},{10,11... | collective-permute-start | bytes 540680 | tf_op jit(solution)/shard_map/ppermute | solution.py:68
  58.6 10.3 %collective-permute-start = (bf16[256,352]{0,1:T(8,128)(2,1)S(1)}, bf16[256,352]{0,1:T(8,128)(2,1)S(1)}, u32[]{:S(2)}, u32[]{:S(2)}) collective-permute-start(bf16[256,352]{0,1:T(8,128)(2,1)S(1)} %bitcast.32), channel_id=1, source_target_pairs={{0,1},{1,0},{2,3},{3,2},{4,5},{5,4},{6,7},{7,6},{8,9},{9,8},{10,11... | collective-permute-start | bytes 540680 | tf_op jit(solution)/shard_map/ppermute | solution.py:68
  69.8 88.0 %all-gather.8.cloned.1.call-start = ((), (), s32[]{:S(2)}) async-start(), calls=%async_computation.8 | async-start | bytes 1802240 | tf_op jit(solution)/shard_map/all_gather | solution.py:76
  69.8 8.9 %copy-start.7 = (s32[2]{0:T(128)S(1)}, s32[2]{0:T(128)}, u32[]{:S(2)}) copy-start(s32[2]{0:T(128)} %param.12) | copy-start | bytes 28
  69.8 7.0 %collective-permute-start.2 = (bf16[352,256]{1,0:T(8,128)(2,1)S(1)}, bf16[352,256]{1,0:T(8,128)(2,1)S(1)}, u32[]{:S(2)}, u32[]{:S(2)}) collective-permute-start(bf16[352,256]{1,0:T(8,128)(2,1)S(1)} %bitcast.33), channel_id=1, source_target_pairs={{0,1},{1,0},{2,3},{3,2},{4,5},{5,4},{6,7},{7,6},{8,9},{9,8},{10,11... | collective-permute-start | bytes 540680 | tf_op jit(solution)/shard_map/ppermute | solution.py:68
  77.7 102.7 %all-gather.6.cloned.1.call-start = ((), (), s32[]{:S(2)}) async-start(), calls=%async_computation.7 | async-start | bytes 1802240 | tf_op jit(solution)/shard_map/all_gather | solution.py:75
  180.4 4.4 %copy-start.9 = (bf16[704,1024]{1,0:T(8,128)(2,1)S(1)}, bf16[704,1024]{1,0:T(8,128)(2,1)}, u32[]{:S(2)}) copy-start(bf16[704,1024]{1,0:T(8,128)(2,1)} %all-gather.8.cloned.1.call-done) | copy-start | bytes 4325380
  184.8 1.0 copy-start.1
  184.8 2.9 copy-start.2
  184.8 1.9 copy-start.10
  186.7 1.4 copy-start.8
  194.7 117.7 %all-to-all-start.2 = ((bf16[128,4,2048]{2,1,0:T(4,128)(2,1)}), bf16[128,4,2048]{2,1,0:T(4,128)(2,1)}, u32[]{:S(2)}, u32[]{:S(2)}) async-start(bf16[128,4,2048]{2,1,0:T(4,128)(2,1)} %reshape.74), calls=%async_computation.2 | async-start | bytes 4194304 | tf_op jit(solution)/shard_map/all_to_all | solution.py:101
  214.0 103.0 %reduce-scatter.4.cloned.1.call-start = ((), (), s32[]{:S(2)}) async-start(), calls=%async_computation.9 | async-start | bytes 901120 | tf_op jit(solution)/shard_map/reduce_scatter | solution.py:112
  216.2 24.0 %collective-permute-start.3 = (bf16[1024,352]{0,1:T(8,128)(2,1)S(1)}, bf16[1024,352]{0,1:T(8,128)(2,1)S(1)}, u32[]{:S(2)}, u32[]{:S(2)}) collective-permute-start(bf16[1024,352]{0,1:T(8,128)(2,1)S(1)} %select_convert_fusion.2), channel_id=1, source_target_pairs={{0,1},{1,0},{2,3},{3,2},{4,5},{5,4},{6,7},{7,6},{8,9},{9,8},{10,11... | collective-permute-start | bytes 2162696 | tf_op jit(solution)/shard_map/ppermute | solution.py:110
  241.6 75.4 %reduce-scatter.6.cloned.1.call-start = ((), (), s32[]{:S(2)}) async-start(), calls=%async_computation.10 | async-start | bytes 901120 | tf_op jit(solution)/shard_map/reduce_scatter | solution.py:113
  243.8 24.4 %collective-permute-start.4 = (bf16[1024,352]{0,1:T(8,128)(2,1)S(1)}, bf16[1024,352]{0,1:T(8,128)(2,1)S(1)}, u32[]{:S(2)}, u32[]{:S(2)}) collective-permute-start(bf16[1024,352]{0,1:T(8,128)(2,1)S(1)} %select_convert_fusion.1), channel_id=1, source_target_pairs={{0,1},{1,0},{2,3},{3,2},{4,5},{5,4},{6,7},{7,6},{8,9},{9,8},{10,11... | collective-permute-start | bytes 2162696 | tf_op jit(solution)/shard_map/ppermute | solution.py:110
  269.5 64.8 %reduce-scatter.8.cloned.1.call-start = ((), (), s32[]{:S(2)}) async-start(), calls=%async_computation.11 | async-start | bytes 901120 | tf_op jit(solution)/shard_map/reduce_scatter | solution.py:114
  270.6 23.5 %collective-permute-start.5 = (bf16[352,1024]{1,0:T(8,128)(2,1)S(1)}, bf16[352,1024]{1,0:T(8,128)(2,1)S(1)}, u32[]{:S(2)}, u32[]{:S(2)}) collective-permute-start(bf16[352,1024]{1,0:T(8,128)(2,1)S(1)} %select_convert_fusion), channel_id=1, source_target_pairs={{0,1},{1,0},{2,3},{3,2},{4,5},{5,4},{6,7},{7,6},{8,9},{9,8},{10,11... | collective-permute-start | bytes 2162696 | tf_op jit(solution)/shard_map/ppermute | solution.py:110
Sparse Core Ops, SparseCore 0:
  69.9 38.4 all-gather.3
  110.5 34.2 all-gather.7
  146.9 33.4 all-gather.5
  241.7 29.6 reduce-scatter.3
  274.7 27.7 reduce-scatter.5
  305.8 28.4 reduce-scatter.7
